TPU v7x, 32 devices: a whole 2x2x4 slice. The times are simulated.
32 devices in a mesh: seq: 8 (over z, y), dp: 4 (over x, core).
Axes of the slice: x: 2, y: 2, z: 4, core: 2. Of those that a mesh axis runs over, the one named last changes fastest.
Arguments:
- out_grad: bfloat16 [4, 1536, 4096], P('dp', 'seq'), may hold values from -6 to 6
- w_out: bfloat16 [2048, 4096], P('dp'), may hold values from -0.125 to 0.125
- queries: bfloat16 [4, 1536, 2048], P('dp', 'seq'), may hold values from -6 to 6
- keys: bfloat16 [4, 1536, 2048], P('dp', 'seq'), may hold values from -6 to 6
- values: bfloat16 [4, 1536, 2048], P('dp', 'seq'), may hold values from -6 to 6
- keep_bits: int32 [4, 1536, 128], P('dp', 'seq'), may hold values from 0 to 65535
- query_later: float32 [4, 16, 128, 128], P('dp'), may hold values from -1.8 to 1.8
Outputs:
- query_grad: bfloat16 [4, 1536, 2048], P('dp', 'seq')
- key_grad: bfloat16 [4, 1536, 2048], P('dp', 'seq')
- value_grad: bfloat16 [4, 1536, 2048], P('dp', 'seq')
All inputs are finite; a program needn't handle non-finite values.
Results may differ from a plain program's by a relative error of at most 0.0058.
Values may be sent and summed in bfloat16 or wider, within the bound.
A program may use at most 192 MiB of HBM per device.

v0:
```python
import jax
import jax.numpy as jnp
from jax import lax
from jax.sharding import PartitionSpec as P

HD = 128


def carried_in(part, axis, combine, identity, reverse):
    count = lax.axis_size(axis)
    place = lax.axis_index(axis)
    ahead = count - 1 - place if reverse else place
    gathered = lax.all_gather(part, axis)
    state = jnp.zeros_like(part) + jnp.asarray(identity, part.dtype)

    def one(step, state):
        source = count - 1 - step if reverse else step
        return combine(state, lax.dynamic_index_in_dim(gathered, source, 0, False))

    return lax.fori_loop(0, ahead, one, state)


def unpack_flags(word_bits, count):
    bit_shift = jnp.arange(16, dtype=jnp.int32)
    flags = word_bits[..., None] >> bit_shift & 1
    return flags.reshape(word_bits.shape[:-1] + (count,)).astype(jnp.float32)


def add_states(earlier, later):
    return earlier + later


def body(out_grad, w_out, queries, keys, values, keep_bits, query_later):
    tok_count = out_grad.shape[1]
    inner_width = queries.shape[2]
    head_size = HD
    head_count = inner_width // head_size
    grad_tokens = out_grad[0]
    projected = lax.dot_general(
        grad_tokens,
        lax.all_gather(w_out, "dp", axis=0, tiled=True),
        (((1,), (1,)), ((), ())),
        preferred_element_type=jnp.float32,
    )
    keep_mask = unpack_flags(keep_bits[0], inner_width)
    position = (lax.axis_index("seq") * tok_count + jnp.arange(tok_count, dtype=jnp.int32)).astype(
        jnp.float32
    )
    row_scale = 2.0 / jnp.sqrt(head_size * (position + 1.0))
    gated = (projected * keep_mask * row_scale[:, None]).astype(jnp.bfloat16)
    gated_heads = gated.reshape(tok_count, head_count, head_size)
    query_heads = queries[0].reshape(tok_count, head_count, head_size)
    key_heads = keys[0].reshape(tok_count, head_count, head_size)
    value_heads = values[0].reshape(tok_count, head_count, head_size)
    key_state = jnp.einsum(
        "thi,thj->hij", key_heads, value_heads, preferred_element_type=jnp.float32
    )
    query_state = jnp.einsum(
        "thi,thj->hij", query_heads, gated_heads, preferred_element_type=jnp.float32
    )
    zero_state = jnp.zeros_like(key_state)
    key_before = carried_in(key_state, "seq", add_states, zero_state, False)
    query_after = carried_in(query_state, "seq", add_states, zero_state, True)
    query_after = query_after + query_later[0]
    key_before_b = key_before.astype(jnp.bfloat16)
    query_after_b = query_after.astype(jnp.bfloat16)
    causal_mask = (jnp.arange(tok_count)[:, None] >= jnp.arange(tok_count)[None, :]).astype(
        jnp.float32
    )
    grad_scores = (
        jnp.einsum("thj,shj->hts", gated_heads, value_heads, preferred_element_type=jnp.float32)
        * causal_mask
    ).astype(jnp.bfloat16)
    attn_scores = (
        jnp.einsum("thj,shj->hts", query_heads, key_heads, preferred_element_type=jnp.float32)
        * causal_mask
    ).astype(jnp.bfloat16)
    query_grad = jnp.einsum(
        "hts,shi->thi", grad_scores, key_heads, preferred_element_type=jnp.float32
    )
    query_grad = query_grad + jnp.einsum(
        "thj,hij->thi", gated_heads, key_before_b, preferred_element_type=jnp.float32
    )
    key_grad = jnp.einsum(
        "hts,thi->shi", grad_scores, query_heads, preferred_element_type=jnp.float32
    )
    key_grad = key_grad + jnp.einsum(
        "shj,hij->shi", value_heads, query_after_b, preferred_element_type=jnp.float32
    )
    value_grad = jnp.einsum(
        "hts,thj->shj", attn_scores, gated_heads, preferred_element_type=jnp.float32
    )
    value_grad = value_grad + jnp.einsum(
        "shi,hij->shj", key_heads, query_after_b, preferred_element_type=jnp.float32
    )

    def merge_heads(tensor):
        return tensor.reshape(1, tok_count, inner_width).astype(jnp.bfloat16)

    return (merge_heads(query_grad), merge_heads(key_grad), merge_heads(value_grad))


def solution(mesh):
    in_specs = (
        P("dp", "seq", None),
        P("dp", None),
        P("dp", "seq", None),
        P("dp", "seq", None),
        P("dp", "seq", None),
        P("dp", "seq", None),
        P("dp", None, None, None),
    )
    out_specs = (P("dp", "seq", None), P("dp", "seq", None), P("dp", "seq", None))
    return jax.shard_map(body, mesh=mesh, in_specs=in_specs, out_specs=out_specs, check_vma=False)
```

profile of v0, /device:TPU:0, one launch (start us, length us, event | category | flops | bytes accessed | tf_op | source)
XLA Modules:
  0.0 395.9 jit_solution(10310405240292140329)
XLA Ops:
  7.2 0.0 copy-start
  7.2 0.0 copy-start.10
  7.2 0.0 all-gather.6.cloned.1.call-start
  7.2 0.7 all-gather.6.cloned.1.call-update
  7.9 0.0 all-gather.8.cloned.1.call-start
  8.0 0.0 copy-start.11
  8.0 0.5 copy-done.10
  8.4 0.2 copy.71
  8.6 0.0 copy-start.2
  8.6 0.6 copy-done.11
  9.2 0.2 copy.70
  9.3 0.0 copy-start.13
  9.3 1.5 fusion.21
  10.9 0.0 copy-done.2
  10.9 0.0 all-gather.8.cloned.1.call-update
  10.9 0.0 all-gather.10.cloned.1.call-start
  11.0 0.0 copy-done.13
  11.0 0.1 copy.45
  11.1 1.6 shift_right_arithmetic.23
  12.6 2.9 copy.46
  15.6 0.1 shift_right_arithmetic.26
  15.6 0.0 copy-done.12
  15.6 1.2 copy.72
  16.8 101.4 %all-gather.6.cloned.1.call-done = bf16[2048,4096]{1,0:T(8,128)(2,1)} async-done(((bf16[512,4096]{1,0:T(8,128)(2,1)}), bf16[2048,4096]{1,0:T(8,128)(2,1)}) %all-gather.6.cloned.1.call-update) | async-done | bytes 16777232 | tf_op jit(solution)/shard_map/all_gather | solution.py:41
  118.2 0.0 copy-done
  118.2 11.9 %fusion.7 = bf16[24,16,8,128]{3,2,1,0:T(8,128)(2,1)S(1)} fusion(s32[192,2048]{1,0:T(8,128)} %copy.46, bf16[2048,4096]{1,0:T(8,128)(2,1)} %all-gather.6.cloned.1.call-done, bf16[1,192,4096]{2,1,0:T(8,128)(2,1)S(1)} %copy-done, f32[192]{0:T(256)S(1)} %rsqrt_multiply_fusion, s32[2048]{0:T(1024)S(1)} %shift_right_arithmetic.26), kind=kOutput, calls=%fused_computation.16 | convolution fusion | flops 3223584768 | bytes 20718336 | tf_op jit(solution)/shard_map/dot_general | solution.py:39
  130.2 0.0 copy-start.6
  130.2 1.9 convolution_bitcast_fusion
  132.1 1.3 copy.58
  133.5 0.0 all-gather.10.cloned.1.call-update
  133.5 0.7 fusion.35
  134.2 111.2 %all-gather.8.cloned.1.call-done = f32[128,128,128]{2,1,0:T(8,128)} async-done(((f32[16,128,128]{2,1,0:T(8,128)}), f32[128,128,128]{2,1,0:T(8,128)}) %all-gather.8.cloned.1.call-update) | async-done | bytes 8388624 | tf_op jit(solution)/shard_map/all_gather | solution.py:13
  245.3 0.1 broadcast_in_dim.2.clone
  245.4 0.0 copy-done.6
  245.5 0.0 copy-start.3
  245.5 1.8 multiply_convert_fusion.1
  247.3 0.0 copy-start.7
  247.3 0.6 fusion.33
  247.9 0.6 copy-done.7
  248.5 0.5 fusion.3
  249.0 0.5 copy.53
  249.5 1.2 convert_element_type.86
  250.7 3.2 fusion.18
  253.9 3.7 fusion.5
  257.6 113.0 %all-gather.10.cloned.1.call-done = f32[128,128,128]{2,1,0:T(8,128)} async-done(((f32[16,128,128]{2,1,0:T(8,128)}), f32[128,128,128]{2,1,0:T(8,128)}) %all-gather.10.cloned.1.call-update) | async-done | bytes 8388624 | tf_op jit(solution)/shard_map/all_gather | solution.py:13
  370.6 0.1 broadcast_in_dim.2.clone.1
  370.7 10.8 %while.23 = (s32[]{:T(128)}, f32[16,128,128]{2,1,0:T(8,128)S(1)}, s32[]{:T(128)}, f32[8,16,128,128]{3,2,1,0:T(8,128)}, s32[]{:T(128)}, /*index=5*/s32[]{:T(128)}, s32[]{:T(128)}, s32[]{:T(128)}) while((s32[]{:T(128)}, f32[16,128,128]{2,1,0:T(8,128)S(1)}, s32[]{:T(128)}, f32[8,16,128,128]{3,2,1,0:T(8,128)}, s32[]{:T(128)}, ...), condition=%wide.region_3.4_spmd, body=%wide.region_2.3_spmd.sunk | while | flops 262150 | bytes 3145863 | solution.py:20
  370.7 1.5 bitcast_add_fusion.8
  372.3 1.5 bitcast_add_fusion.8
  373.8 1.5 bitcast_add_fusion.8
  375.3 1.5 bitcast_add_fusion.8
  376.8 1.5 bitcast_add_fusion.8
  378.3 1.5 bitcast_add_fusion.8
  379.8 1.5 bitcast_add_fusion.8
  381.5 0.0 copy-start.5
  381.5 1.5 fusion.10
  383.0 0.0 copy-done.5
  383.1 0.4 copy-done.8
  383.5 0.4 fusion.6
  383.9 0.5 copy.66
  384.4 1.2 convert_element_type.93
  385.6 2.0 fusion.2
  387.6 0.5 copy.60
  388.1 1.2 convert_element_type.89
  (12 shorter events, 0.0 us)
Async XLA Ops:
  7.2 111.1 %copy-start = (bf16[1,192,4096]{2,1,0:T(8,128)(2,1)S(1)}, bf16[1,192,4096]{2,1,0:T(8,128)(2,1)}, u32[]{:S(2)}) copy-start(bf16[1,192,4096]{2,1,0:T(8,128)(2,1)} %param.11) | copy-start | bytes 4718596
  7.2 1.3 copy-start.10
  7.2 111.0 %all-gather.6.cloned.1.call-start = ((), (), s32[]{:S(2)}) async-start(), calls=%async_computation | async-start | bytes 20971520 | tf_op jit(solution)/shard_map/all_gather | solution.py:41
  7.9 237.4 %all-gather.8.cloned.1.call-start = ((), (), s32[]{:S(2)}) async-start(), calls=%async_computation.1 | async-start | bytes 9437184 | tf_op jit(solution)/shard_map/all_gather | solution.py:13
  8.0 1.2 copy-start.11
  8.6 2.3 copy-start.2
  9.3 1.6 copy-start.13
  10.9 359.7 %all-gather.10.cloned.1.call-start = ((), (), s32[]{:S(2)}) async-start(), calls=%async_computation.2 | async-start | bytes 9437184 | tf_op jit(solution)/shard_map/all_gather | solution.py:13
  12.6 3.0 copy-start.12
  130.2 115.3 %copy-start.6 = (bf16[24,16,8,128]{3,2,1,0:T(8,128)(2,1)}, bf16[24,16,8,128]{3,2,1,0:T(8,128)(2,1)S(1)}, u32[]{:S(2)}) copy-start(bf16[24,16,8,128]{3,2,1,0:T(8,128)(2,1)S(1)} %fusion.7) | copy-start | bytes 2359300
  245.5 1.9 copy-start.3
  247.3 1.1 copy-start.7
  250.7 3.2 copy-start.4
  250.7 3.2 copy-start.9
  381.5 1.5 copy-start.5
  381.5 2.0 copy-start.8
  385.6 3.7 copy-start.1
Sparse Core Ops, SparseCore 0:
  9.6 108.6 all-gather.5
  120.4 124.9 all-gather.7
  247.5 123.1 all-gather.9
where the time goes:
time: 397 us; the launch traced here: 396 us
  waiting for transfers between devices  326 us (82%)
  matrix products  27.6 us (7%)
  local copies, waits for them, and re-layouts  14.9 us (4%)
  between operations  14 us (4%)
  other arithmetic  12.6 us (3%)
    all_gather x2, waiting for transfers between devices, carried_in(): gathered = lax.all_gather(part, axis)  224 us
    all_gather x1, waiting for transfers between devices, body(): lax.all_gather(w_out, 'dp', axis=0, tiled=True)  101 us
    dot_general x1, matrix products, body(): lax.dot_general(grad_tokens, lax.all_gather(w_out, 'dp', axis=0, tiled=Tr...  11.9 us
    add x7, other arithmetic, add_states(): return earlier + later  10.4 us
  transfers between devices with their start and end apart: 3, of which 3 were waited for; matrix products, arithmetic and copies ran while one was open for 9% of the time, Pallas kernels for 0%

commit v1 on v0

--- a/solution.py
+++ b/solution.py
@@ -4,6 +4,18 @@
 from jax.sharding import PartitionSpec as P
 
 HD = 128
+
+
+def collect(value, axis, dim):
+    ways, here = (lax.axis_size(axis), lax.axis_index(axis))
+    grown, reach = (value, 1)
+    while reach < ways:
+        theirs = lax.ppermute(grown, axis, [(d, d ^ reach) for d in range(ways)])
+        mine_first = jnp.concatenate([grown, theirs], axis=dim)
+        theirs_first = jnp.concatenate([theirs, grown], axis=dim)
+        grown = jnp.where(here & reach == 0, mine_first, theirs_first)
+        reach = 2 * reach
+    return grown
 
 
 def carried_in(part, axis, combine, identity, reverse):
@@ -38,7 +50,7 @@
     grad_tokens = out_grad[0]
     projected = lax.dot_general(
         grad_tokens,
-        lax.all_gather(w_out, "dp", axis=0, tiled=True),
+        collect(w_out, "dp", 0),
         (((1,), (1,)), ((), ())),
         preferred_element_type=jnp.float32,
     )

time: 397 us -> 380 us (0.957)
  waiting for transfers between devices: 326 us -> 291 us
  other arithmetic: 12.6 us -> 23.6 us
    ppermute x0 -> x2, waiting for transfers between devices: none -> 177 us  [collect(): theirs = lax.ppermute(grown, axis, [(d, d ^ reach) for d in range(ways)])]
    all_gather x2, waiting for transfers between devices: 224 us -> 113 us  [carried_in(): gathered = lax.all_gather(part, axis)]
    all_gather x1 -> x0, waiting for transfers between devices: 101 us -> none  [body(): lax.all_gather(w_out, 'dp', axis=0, tiled=True)]
    select_n x0 -> x1, other arithmetic: none -> 11.7 us  [collect(): grown = jnp.where(here & reach == 0, mine_first, theirs_first)]
  transfers between devices with their start and end apart: 3 -> 4, of which waited for: 3 -> 3; matrix products, arithmetic and copies ran while one was open for 9% -> 14% of each run, Pallas kernels for 0% -> 0%
where the time goes in v1:
time: 380 us; the launch traced here: 379 us
  waiting for transfers between devices  291 us (77%)
  matrix products  29.6 us (8%)
  other arithmetic  23.6 us (6%)
  local copies, waits for them, and re-layouts  17.4 us (5%)
  between operations  14.2 us (4%)
    ppermute x2, waiting for transfers between devices, collect(): theirs = lax.ppermute(grown, axis, [(d, d ^ reach) for d in range(ways)])  177 us
    all_gather x2, waiting for transfers between devices, carried_in(): gathered = lax.all_gather(part, axis)  113 us
    dot_general x1, matrix products, body(): lax.dot_general(grad_tokens, collect(w_out, 'dp', 0), (((1,), (1,)), ((),...  13.7 us
    select_n x1, other arithmetic, collect(): grown = jnp.where(here & reach == 0, mine_first, theirs_first)  11.7 us
    add x7, other arithmetic, add_states(): return earlier + later  10.4 us
  transfers between devices with their start and end apart: 4, of which 3 were waited for; matrix products, arithmetic and copies ran while one was open for 14% of the time, Pallas kernels for 0%

profile of v1, /device:TPU:0, one launch (start us, length us, event | category | flops | bytes accessed | tf_op | source)
XLA Modules:
  0.0 379.2 jit_solution(15412036983045742754)
XLA Ops:
  7.2 0.0 copy-start
  7.2 0.0 all-gather.5.cloned.1.call-start
  7.2 0.5 collective-permute-start
  7.7 1.3 copy.70
  9.0 1.3 copy.71
  10.3 1.5 fusion.30
  11.9 0.0 all-gather.5.cloned.1.call-update
  11.9 0.0 all-gather.7.cloned.1.call-start
  12.0 0.0 copy-start.7
  12.0 2.9 collective-permute-done
  14.9 11.7 %maximum_select_fusion.2 = bf16[1024,4096]{1,0:T(8,128)(2,1)} fusion(bf16[512,4096]{1,0:T(8,128)(2,1)} %collective-permute-done, bf16[512,4096]{1,0:T(8,128)(2,1)} %param.12, pred[]{:T(512)S(6)} %eq.7), kind=kLoop, calls=%fused_computation.10 | loop fusion | flops 37748736 | bytes 16777216 | tf_op jit(solution)/shard_map/jit(_where)/select_n | solution.py:16
  26.6 2.9 collective-permute-start.1
  29.4 0.0 copy-done.7
  29.4 0.1 copy.45
  29.5 1.5 shift_right_arithmetic.23
  31.1 2.8 copy.46
  33.8 0.1 shift_right_arithmetic.26
  33.9 2.2 copy.72
  36.1 0.0 copy-start.3
  36.1 174.3 %collective-permute-done.1 = bf16[1024,4096]{1,0:T(8,128)(2,1)} collective-permute-done((bf16[1024,4096]{1,0:T(8,128)(2,1)}, bf16[1024,4096]{1,0:T(8,128)(2,1)}, u32[]{:S(2)}, u32[]{:S(2)}) %collective-permute-start.1) | collective-permute-done | bytes 8388640 | tf_op jit(solution)/shard_map/ppermute | solution.py:13
  210.5 0.0 copy-done
  210.5 13.7 %fusion.16 = bf16[24,16,8,128]{3,2,1,0:T(8,128)(2,1)S(1)} fusion(s32[192,2048]{1,0:T(8,128)} %copy.46, bf16[1,192,4096]{2,1,0:T(8,128)(2,1)S(1)} %copy-done, bf16[1024,4096]{1,0:T(8,128)(2,1)} %collective-permute-done.1, bf16[1024,4096]{1,0:T(8,128)(2,1)} %maximum_select_fusion.2, pred[]{:T(512)S(6)} %eq.6, f32[192]{0:T(256)S(1)} %rsqrt_multiply_fusion, ...), kind=kOutput, calls=%fused_computation.26 | convolution fusion | flops 3299082240 | bytes 20718336 | tf_op jit(solution)/shard_map/dot_general | solution.py:51
  224.1 0.0 copy-start.2
  224.2 0.9 copy-done.2
  225.0 0.0 copy-done.3
  225.0 0.5 convolution_bitcast_fusion
  225.5 1.3 copy.58
  226.9 0.0 all-gather.7.cloned.1.call-update
  226.9 0.0 copy-start.4
  226.9 1.8 multiply_convert_fusion.1
  228.7 1.7 fusion.42
  230.5 0.0 copy-done.4
  230.5 1.9 fusion.27
  232.4 3.6 fusion.14
  236.0 0.0 all-gather.5.cloned.1.call-done
  236.0 0.1 broadcast_in_dim.2.clone
  236.1 2.4 fusion.12
  238.5 0.5 copy.53
  239.0 1.2 convert_element_type.86
  240.3 113.3 %all-gather.7.cloned.1.call-done = f32[128,128,128]{2,1,0:T(8,128)} async-done(((f32[16,128,128]{2,1,0:T(8,128)}), f32[128,128,128]{2,1,0:T(8,128)}) %all-gather.7.cloned.1.call-update) | async-done | bytes 8388624 | tf_op jit(solution)/shard_map/all_gather | solution.py:25
  353.6 0.1 broadcast_in_dim.2.clone.1
  353.7 10.8 %while.23 = (s32[]{:T(128)}, f32[16,128,128]{2,1,0:T(8,128)S(1)}, s32[]{:T(128)}, f32[8,16,128,128]{3,2,1,0:T(8,128)}, s32[]{:T(128)}, /*index=5*/s32[]{:T(128)}, s32[]{:T(128)}, s32[]{:T(128)}) while((s32[]{:T(128)}, f32[16,128,128]{2,1,0:T(8,128)S(1)}, s32[]{:T(128)}, f32[8,16,128,128]{3,2,1,0:T(8,128)}, s32[]{:T(128)}, ...), condition=%wide.region_3.4_spmd, body=%wide.region_2.3_spmd.sunk | while | flops 262150 | bytes 3145871 | solution.py:32
  353.7 1.5 bitcast_add_fusion.8
  355.2 1.5 bitcast_add_fusion.8
  356.7 1.5 bitcast_add_fusion.8
  358.2 1.5 bitcast_add_fusion.8
  359.7 1.5 bitcast_add_fusion.8
  361.3 1.5 bitcast_add_fusion.8
  362.8 1.5 bitcast_add_fusion.8
  364.4 0.0 copy-start.5
  364.5 1.5 fusion.19
  365.9 0.2 copy-done.5
  366.2 0.0 copy-start.6
  366.2 0.5 fusion.11
  366.7 0.3 copy-done.6
  367.0 0.5 copy.60
  367.5 0.0 copy-start.1
  367.5 1.2 convert_element_type.89
  368.7 1.9 fusion.15
  370.7 0.5 copy.66
  371.2 1.2 convert_element_type.93
  372.4 0.0 copy-done.1
  (4 shorter events, 0.0 us)
Async XLA Ops:
  7.2 203.3 %copy-start = (bf16[1,192,4096]{2,1,0:T(8,128)(2,1)S(1)}, bf16[1,192,4096]{2,1,0:T(8,128)(2,1)}, u32[]{:S(2)}) copy-start(bf16[1,192,4096]{2,1,0:T(8,128)(2,1)} %param.11) | copy-start | bytes 4718596
  7.2 228.8 %all-gather.5.cloned.1.call-start = ((), (), s32[]{:S(2)}) async-start(), calls=%async_computation | async-start | bytes 9437184 | tf_op jit(solution)/shard_map/all_gather | solution.py:25
  7.2 7.6 %collective-permute-start = (bf16[512,4096]{1,0:T(8,128)(2,1)}, bf16[512,4096]{1,0:T(8,128)(2,1)}, u32[]{:S(2)}, u32[]{:S(2)}) collective-permute-start(bf16[512,4096]{1,0:T(8,128)(2,1)} %param.12), channel_id=1, source_target_pairs={{0,1},{1,0},{2,3},{3,2},{4,5},{5,4},{6,7},{7,6},{8,9},{9,8},{10,11... | collective-permute-start | bytes 12582920 | tf_op jit(solution)/shard_map/ppermute | solution.py:13
  11.9 341.7 %all-gather.7.cloned.1.call-start = ((), (), s32[]{:S(2)}) async-start(), calls=%async_computation.1 | async-start | bytes 9437184 | tf_op jit(solution)/shard_map/all_gather | solution.py:25
  12.0 17.5 %copy-start.7 = (s32[1,192,128]{2,1,0:T(8,128)S(1)}, s32[1,192,128]{2,1,0:T(8,128)}, u32[]{:S(2)}) copy-start(s32[1,192,128]{2,1,0:T(8,128)} %param.16) | copy-start | bytes 294916
  26.6 183.9 %collective-permute-start.1 = (bf16[1024,4096]{1,0:T(8,128)(2,1)}, bf16[1024,4096]{1,0:T(8,128)(2,1)}, u32[]{:S(2)}, u32[]{:S(2)}) collective-permute-start(bf16[1024,4096]{1,0:T(8,128)(2,1)} %maximum_select_fusion.2), channel_id=1, source_target_pairs={{0,2},{1,3},{2,0},{3,1},{4,6},{5,7},{6,4},{7,5},{8,10},{9,11},{10,... | collective-permute-start | bytes 25165832 | tf_op jit(solution)/shard_map/ppermute | solution.py:13
  36.1 188.9 %copy-start.3 = (bf16[24,8,16,128]{3,2,1,0:T(8,128)(2,1)S(1)}, bf16[24,8,16,128]{3,2,1,0:T(8,128)(2,1)}, u32[]{:S(2)}) copy-start(bf16[24,8,16,128]{3,2,1,0:T(8,128)(2,1)} %copy.72) | copy-start | bytes 2359300
  224.1 0.9 copy-start.2
  226.9 3.6 copy-start.4
  364.4 1.7 copy-start.5
  366.2 0.8 copy-start.6
  367.5 4.9 %copy-start.1 = (bf16[1,192,4096]{2,1,0:T(8,128)(2,1)S(1)}, bf16[1,192,4096]{2,1,0:T(8,128)(2,1)}, u32[]{:S(2)}) copy-start(bf16[1,192,4096]{2,1,0:T(8,128)(2,1)} %param.11) | copy-start | bytes 4718596
Sparse Core Ops, SparseCore 0:
  12.0 127.3 all-gather.4
  227.0 126.5 all-gather.6
